TPU v7x, 32 devices: a whole 2x2x4 slice. The times are simulated.
32 devices in a mesh: wave: 16 (over z, y, x), field: 2 (over core).
Axes of the slice: x: 2, y: 2, z: 4, core: 2. Of those that a mesh axis runs over, the one named last changes fastest.
Arguments:
- right_vector: float32 [4, 3, 512, 2, 512], P('field', None, 'wave'), may hold values from -8 to 8
- left_prev: float32 [4, 3, 512, 2, 512], P('field', None, 'wave'), may hold values from -6 to 6
- beta_prev: float32 [1], replicated, may hold values from 0.5 to 2
- kept_vectors: bfloat16 [20, 4, 3, 512, 2, 512], P(None, 'field', None, 'wave'), may hold values from -8 to 8
- kept_count: int32 [1], replicated, may hold values from 1 to 20
- wave_table: int32 [512], replicated, may hold values from 0 to 511, each once
- legendre: float32 [512, 512, 512], P('wave'), may hold values from -0.25 to 0.25
- quad_weights: float32 [512], replicated, may hold values from 0.2 to 1
- coef_value: bfloat16 [3, 3, 512, 1024], P(None, None, 'wave'), may hold values from -2.390625 to 2.390625
- coef_zonal: bfloat16 [3, 3, 512, 1024], P(None, None, 'wave'), may hold values from -2.390625 to 2.390625
Outputs:
- left_vector: float32 [4, 3, 512, 2, 512], P('field', None, 'wave')
- right_next: float32 [4, 3, 512, 2, 512], P('field', None, 'wave')
- correlations: float32 [20], replicated
- norms: float32 [2], replicated
Inputs may be any that keep to these rules, and one draw needn't show every extreme that they name: The stored vectors numbered below kept_count take part. A permutation: spectral slot s holds zonal wavenumber wave_table[s].
All inputs are finite; a program needn't handle non-finite values.
Results may differ from a plain program's by a relative error of at most 0.0003.
Values sent between devices are 32-bit elements; how exact they have to be, the bound alone decides.
A program may use at most 192 MiB of HBM per device.

v0:
```python
import math

import jax
import jax.numpy as jnp
from jax import lax
from jax.sharding import PartitionSpec as P

time_step = 0.5
epsilon = 1e-06
highest = lax.Precision.HIGHEST


def fourier_tables(wave_table, longitudes, wave_count):
    column = jnp.arange(longitudes, dtype=jnp.int32)
    phase_index = wave_table[:, None] * column[None, :] % longitudes
    angle_rows = phase_index.astype(jnp.float32) * (2.0 * math.pi / longitudes)
    cosine = jnp.cos(angle_rows)
    sine_rows = jnp.sin(angle_rows)
    factor = wave_count ** (-0.5)
    slope_scale = (wave_table.astype(jnp.float32) / wave_count * factor)[:, None, None]
    value_rows = jnp.stack([cosine, -sine_rows], axis=1) * factor
    slope_rows = jnp.stack([-sine_rows, -cosine], axis=1) * slope_scale
    synthesis = jnp.stack([value_rows, slope_rows], axis=2)
    analysis = jnp.stack([cosine, -sine_rows], axis=1) * longitudes ** (-0.5)
    return (synthesis, analysis)


def body(
    right_vector,
    left_prev,
    beta_prev,
    kept_vectors,
    kept_count,
    wave_table,
    legendre,
    quad_weights,
    coef_value,
    coef_zonal,
):
    levels = right_vector.shape[0]
    fields = right_vector.shape[1]
    waves_dev = legendre.shape[0]
    degrees = legendre.shape[1]
    lat_dev = coef_value.shape[2]
    longitudes = coef_value.shape[3]
    groups = lax.axis_size("wave")
    keep_count = kept_vectors.shape[0]
    entries = float(right_vector.size * groups * lax.axis_size("field"))
    device = lax.axis_index("wave")
    own_waves = lax.dynamic_slice_in_dim(wave_table, device * waves_dev, waves_dev)
    degree_ids = jnp.arange(degrees, dtype=jnp.int32)
    live_mask = (degree_ids[None, :] >= own_waves[:, None]).astype(jnp.float32)
    wide_mask = live_mask[None, None, :, None, :]
    own_weights = lax.dynamic_slice_in_dim(quad_weights, device * lat_dev, lat_dev)[
        None, None, :, None
    ]
    synthesis, analysis = fourier_tables(wave_table, longitudes, degrees)
    synthesis = synthesis.reshape(groups, waves_dev, 2, 2, longitudes)
    analysis = analysis.reshape(groups, waves_dev, 2, longitudes)
    blocked = legendre.reshape(waves_dev, degrees, groups, lat_dev)
    value_coef = coef_value.astype(jnp.float32)
    zonal_coef = coef_zonal.astype(jnp.float32)

    def to_latitudes(spectral):
        latitude_part = jnp.einsum("lfsrn,snwt->lwftsr", spectral, blocked, precision=highest)
        return latitude_part.reshape(levels, groups, fields * lat_dev * waves_dev * 2)

    def to_degrees(gathered):
        spectral = jnp.einsum("lwftsr,snwt->lfsrn", gathered, blocked, precision=highest)
        return spectral * wide_mask

    right_live = right_vector * wide_mask
    prev_live = left_prev * wide_mask
    block_in = lax.all_to_all(
        to_latitudes(right_live), "wave", split_axis=1, concat_axis=1, tiled=True
    )
    item_count = block_in.shape[0]
    spread = block_in.reshape(item_count, groups, fields, lat_dev, waves_dev, 2)
    grid_values = jnp.einsum("iwftsr,wsrkx->ikftx", spread, synthesis, precision=highest)
    tendency = jnp.sum(value_coef[None] * grid_values[:, 0, None], axis=2)
    tendency = tendency + jnp.sum(zonal_coef[None] * grid_values[:, 1, None], axis=2)
    weighted = tendency * own_weights
    outgoing = jnp.einsum("iftx,wsrx->iwftsr", weighted, analysis, precision=highest)
    returned = lax.all_to_all(
        outgoing.reshape(item_count, groups, -1), "wave", split_axis=1, concat_axis=1, tiled=True
    )
    gathered = returned.reshape(item_count, groups, fields, lat_dev, waves_dev, 2)
    residual_left = right_live + time_step * to_degrees(gathered) - beta_prev[0] * prev_live
    kept_live = (kept_vectors.astype(jnp.float32) * wide_mask[None]).reshape(keep_count, -1)
    live_flags = (jnp.arange(keep_count, dtype=jnp.int32) < kept_count[0]).astype(jnp.float32)

    def project(vector):
        return jnp.dot(kept_live, vector.reshape(-1), precision=highest)

    block_in = lax.all_to_all(
        to_latitudes(residual_left), "wave", split_axis=1, concat_axis=1, tiled=True
    )
    item_count = block_in.shape[0]
    spread = block_in.reshape(item_count, groups, fields, lat_dev, waves_dev, 2)
    weighted = jnp.einsum("iwftsr,wsrx->iftx", spread, analysis, precision=highest) * own_weights
    value_part = jnp.sum(value_coef[None] * weighted[:, :, None], axis=1)
    zonal_part = jnp.sum(zonal_coef[None] * weighted[:, :, None], axis=1)
    stacked = jnp.stack([value_part, zonal_part], axis=1)
    outgoing = jnp.einsum("ikftx,wsrkx->iwftsr", stacked, synthesis, precision=highest)
    returned = lax.all_to_all(
        outgoing.reshape(item_count, groups, -1), "wave", split_axis=1, concat_axis=1, tiled=True
    )
    gathered = returned.reshape(item_count, groups, fields, lat_dev, waves_dev, 2)
    adjoint_raw = residual_left + time_step * to_degrees(gathered)
    totals = lax.psum(
        (
            jnp.sum(residual_left * residual_left),
            jnp.sum(adjoint_raw * adjoint_raw),
            jnp.sum(adjoint_raw * right_live),
            jnp.sum(right_live * right_live),
            project(adjoint_raw),
            project(right_live),
            jnp.dot(kept_live, kept_live.T, precision=highest),
        ),
        ("wave", "field"),
    )
    left_square, image_square, image_cross, right_square, kept_image, kept_right, gram_matrix = [
        summed / entries for summed in totals
    ]
    alpha_norm = jnp.sqrt(left_square + epsilon)
    left_vector = residual_left / alpha_norm
    raw_correlation = kept_image / alpha_norm - alpha_norm * kept_right
    correlations = raw_correlation * live_flags
    square = (
        image_square / (alpha_norm * alpha_norm)
        - 2.0 * image_cross
        + alpha_norm * alpha_norm * right_square
    )
    square = (
        square
        - 2.0 * jnp.sum(correlations * raw_correlation)
        + jnp.dot(
            correlations, jnp.dot(gram_matrix, correlations, precision=highest), precision=highest
        )
    )
    beta_norm = jnp.sqrt(square + epsilon)
    orthogonal = (
        adjoint_raw / alpha_norm
        - alpha_norm * right_live
        - jnp.dot(correlations, kept_live, precision=highest).reshape(right_live.shape)
    )
    return (left_vector, orthogonal / beta_norm, correlations, jnp.stack([alpha_norm, beta_norm]))


def solution(mesh):
    return jax.shard_map(
        body,
        mesh=mesh,
        in_specs=(
            P("field", None, "wave", None, None),
            P("field", None, "wave", None, None),
            P(),
            P(None, "field", None, "wave", None, None),
            P(),
            P(),
            P("wave", None, None),
            P(),
            P(None, None, "wave", None),
            P(None, None, "wave", None),
        ),
        out_specs=(
            P("field", None, "wave", None, None),
            P("field", None, "wave", None, None),
            P(),
            P(),
        ),
        check_vma=False,
    )
```

profile of v0, /device:TPU:0, one launch (start us, length us, event | category | flops | bytes accessed | tf_op | source)
XLA Modules:
  0.0 760.5 jit_solution(3930852589484011653)
XLA Ops:
  1.5 33.4 %copy.73 = f32[32,512,512]{1,2,0:T(8,128)} copy(f32[32,512,512]{2,1,0:T(8,128)} %param.16) | data formatting | bytes 67108864 | tf_op args[6]
  34.9 86.2 %convolution_bitcast_fusion.1 = f32[2,16,3,32,32,2]{3,2,1,5,0,4:T(4,128)} fusion(f32[32,512,16,32,1,1]{1,3,2,5,4,0:T(8,128)} %bitcast.179, f32[2,3,32,2,512]{4,3,2,1,0:T(2,128)S(1)} %copy-done.1, f32[32,512]{1,0:T(8,128)S(1)} %fusion.74), kind=kOutput, calls=%fused_computation.31 | convolution fusion | flops 1208156160 | bytes 35192832 | tf_op jit(solution)/shard_map/lfsrn,snwt->lwftsr/dot_general | solution.py:65
  121.2 9.5 %copy.74 = f32[2,16,3,32,32,2]{1,5,4,3,2,0:T(2,128)} copy(f32[2,16,3,32,32,2]{3,2,1,5,0,4:T(4,128)} %convolution_bitcast_fusion.1) | data formatting | bytes 1572864 | tf_op jit(solution)/shard_map/lfsrn,snwt->lwftsr/transpose | solution.py:65
  130.7 5.4 copy.75
  136.1 8.4 %all-to-all-start = ((f32[2,16,6144]{2,0,1:T(2,128)}), f32[2,16,6144]{2,0,1:T(2,128)}, u32[]{:S(2)}, u32[]{:S(2)}) async-start(f32[2,16,6144]{2,0,1:T(2,128)} %copy.75), calls=%async_computation | async-start | bytes 1572864 | tf_op jit(solution)/shard_map/all_to_all | solution.py:74
  146.7 10.7 %fusion.62 = (f32[16,32,1,1,1024]{4,1,0,3,2:T(8,128)S(1)}, f32[16,32,1,1,1024]{4,1,0,3,2:T(8,128)S(1)}, f32[16,32,1,1,1024]{4,1,0,2,3:T(8,128)S(1)}, f32[16,32,1...) fusion(s32[16,32]{1,0:T(8,128)S(1)} %mul.312), kind=kLoop, calls=%fused_computation.76 | loop fusion | flops 8388608 | bytes 12584960 | tf_op jit(solution)/shard_map/stack | solution.py:24
  169.1 9.6 %copy.77 = f32[2,16,3,32,32,2]{4,3,1,5,2,0:T(8,128)} copy(f32[2,16,3,32,32,2]{1,5,4,3,2,0:T(2,128)} %bitcast.187) | data formatting | bytes 1572864 | tf_op jit(solution)/shard_map/reshape | solution.py:78
  178.7 9.6 %fusion.32 = f32[2,2,3,32,1024]{4,3,2,0,1:T(8,128)S(1)} fusion(f32[2,16,3,32,32,2]{4,3,1,5,2,0:T(8,128)} %copy.77, f32[16,32,2,1,1024]{4,1,0,2,3:T(8,128)} %maximum_multiply_fusion.2, f32[16,32,2,1,1024]{4,1,0,2,3:T(8,128)} %fusion.14), kind=kOutput, calls=%fused_computation.45 | convolution fusion | flops 4833935360 | bytes 10747904 | tf_op jit(solution)/shard_map/iwftsr,wsrkx->ikftx/dot_general | solution.py:79
  190.5 11.8 %fusion.24 = f32[2,16,3,32,32,2]{3,4,2,0,5,1:T(8,128)} fusion(f32[2,3,32,1024]{3,2,1,0:T(8,128)S(1)} %get-tuple-element.46, f32[2,3,32,1024]{3,2,1,0:T(8,128)S(1)} %get-tuple-element.45, f32[32]{0:T(128)S(1)} %dynamic_slice.7, f32[16,32,1,1024]{3,1,0,2:T(8,128)S(1)} %copy-done.8, f32[16,32,1,1024]{3,1,0,2:T(8,128)S(1)} %copy-done.9), kind=kOutput, calls=%fused_computation.40 | convolution fusion | flops 2418409472 | bytes 6553728 | tf_op jit(solution)/shard_map/iftx,wsrx->iwftsr/dot_general | solution.py:83
  202.2 10.9 %copy.79 = f32[2,16,3,32,32,2]{1,5,4,3,2,0:T(2,128)} copy(f32[2,16,3,32,32,2]{3,4,2,0,5,1:T(8,128)} %fusion.24) | data formatting | bytes 1572864 | tf_op jit(solution)/shard_map/iftx,wsrx->iwftsr/transpose | solution.py:83
  213.2 5.3 copy.80
  218.5 5.4 all-to-all-start.1
  224.6 18.5 %all-to-all-done.1 = f32[2,16,6144]{2,0,1:T(2,128)} async-done(((f32[2,16,6144]{2,0,1:T(2,128)}), f32[2,16,6144]{2,0,1:T(2,128)}, u32[]{:S(2)}, u32[]{:S(2)}) %all-to-all-start.1) | async-done | bytes 786464 | tf_op jit(solution)/shard_map/all_to_all | solution.py:84
  247.9 9.8 %copy.82 = f32[2,16,3,32,32,2]{3,2,1,5,0,4:T(4,128)} copy(f32[2,16,3,32,32,2]{1,5,4,3,2,0:T(2,128)} %bitcast.189) | data formatting | bytes 1572864 | tf_op jit(solution)/shard_map/reshape | solution.py:87
  257.7 37.0 %multiply_reduce_fusion.7 = (f32[]{:T(128)}, f32[2,3,32,2,512]{4,1,3,0,2:T(4,128)S(1)}) fusion(f32[2,3,32,2,512]{4,3,2,1,0:T(2,128)} %param.11, f32[]{:T(128)} %bitcast.177, f32[32,512]{1,0:T(8,128)S(1)} %fusion.74, f32[2,16,3,32,32,2]{3,2,1,5,0,4:T(4,128)} %copy.82, f32[32,512,16,32,1,1]{1,3,2,5,4,0:T(8,128)} %bitcast.180, ...), kind=kOutput, calls=%fused_computation.74 | convolution fusion | flops 1209729024 | bytes 36765704 | tf_op jit(solution)/shard_map/lwftsr,snwt->lfsrn/dot_general | solution.py:69
  295.7 75.5 %convolution_bitcast_fusion = f32[2,16,3,32,32,2]{3,2,1,5,0,4:T(4,128)} fusion(f32[32,512,16,32,1,1]{1,3,2,5,4,0:T(8,128)} %bitcast.181, f32[2,3,32,2,512]{4,1,3,0,2:T(4,128)S(1)} %get-tuple-element.44), kind=kOutput, calls=%fused_computation.30 | convolution fusion | flops 1207959552 | bytes 35127296 | tf_op jit(solution)/shard_map/lfsrn,snwt->lwftsr/dot_general | solution.py:65
  371.2 9.5 %copy.84 = f32[2,16,3,32,32,2]{1,5,4,3,2,0:T(2,128)} copy(f32[2,16,3,32,32,2]{3,2,1,5,0,4:T(4,128)} %convolution_bitcast_fusion) | data formatting | bytes 1572864 | tf_op jit(solution)/shard_map/lfsrn,snwt->lwftsr/transpose | solution.py:65
  385.2 25.1 %all_to_all.20 = f32[2,16,6144]{2,0,1:T(2,128)} all-to-all(f32[2,16,6144]{2,0,1:T(2,128)S(1)} %copy.85), channel_id=1, replica_groups=mesh['wave'=16,'field'=2] {'wave'}, dimensions={1} | all-to-all | bytes 1572864 | tf_op jit(solution)/shard_map/all_to_all | solution.py:95
  415.2 9.6 %copy.87 = f32[2,16,3,32,32,2]{4,3,1,5,2,0:T(8,128)} copy(f32[2,16,3,32,32,2]{1,5,4,3,2,0:T(2,128)} %bitcast.191) | data formatting | bytes 1572864 | tf_op jit(solution)/shard_map/reshape | solution.py:99
  424.7 7.9 %fusion.37 = f32[2,3,32,1024]{3,2,1,0:T(8,128)S(1)} fusion(f32[2,16,3,32,32,2]{4,3,1,5,2,0:T(8,128)} %copy.87, f32[32]{0:T(128)S(1)} %dynamic_slice.7, f32[16,32,1,1024]{3,1,0,2:T(8,128)} %get-tuple-element.41, f32[16,32,1,1024]{3,1,0,2:T(8,128)} %get-tuple-element.42), kind=kOutput, calls=%fused_computation.49 | convolution fusion | flops 2418212864 | bytes 5767296 | tf_op jit(solution)/shard_map/iwftsr,wsrx->iftx/dot_general | solution.py:100
  434.8 20.4 %fusion.27 = f32[2,16,3,32,32,2]{3,4,2,0,5,1:T(8,128)S(1)} fusion(f32[2,1,3,32,1024]{4,3,1,2,0:T(8,128)S(1)} %bitcast.196, f32[2,1,3,32,1024]{4,3,1,2,0:T(8,128)S(1)} %bitcast.195, f32[16,32,2,1,1024]{4,1,0,2,3:T(8,128)S(1)} %copy-done.6, f32[16,32,2,1,1024]{4,1,0,2,3:T(8,128)S(1)} %copy-done.7), kind=kOutput, calls=%fused_computation.41 | convolution fusion | flops 4834328576 | bytes 10747904 | tf_op jit(solution)/shard_map/ikftx,wsrkx->iwftsr/dot_general | solution.py:104
  455.3 8.1 %copy.89 = f32[2,16,3,32,32,2]{1,5,4,3,2,0:T(2,128)} copy(f32[2,16,3,32,32,2]{3,4,2,0,5,1:T(8,128)S(1)} %fusion.27) | data formatting | bytes 1572864 | tf_op jit(solution)/shard_map/ikftx,wsrkx->iwftsr/transpose | solution.py:104
  472.5 8.7 %convert_multiply_fusion = f32[20,2,3,32,2,512]{5,4,3,2,1,0:T(2,128)} fusion(bf16[20,2,3,32,2,512]{5,4,3,2,1,0:T(2,128)(2,1)} %param.13, f32[32,512]{1,0:T(8,128)S(1)} %fusion.74), kind=kLoop, calls=%fused_computation.8 | loop fusion | flops 7864320 | bytes 23658496 | tf_op jit(solution)/shard_map/mul | solution.py:89
  481.9 30.3 %reshape.276 = f32[20,196608]{1,0:T(8,128)} reshape(f32[20,2,3,32,2,512]{5,4,3,2,1,0:T(2,128)} %convert_multiply_fusion) | data formatting | bytes 31457280 | tf_op jit(solution)/shard_map/reshape | solution.py:89
  512.2 29.0 %dot_general.57 = f32[2,3,32,2,512,20]{4,3,2,1,0,5:T(2,128)} reshape(f32[196608,20]{0,1:T(8,128)} %bitcast.185) | data formatting | bytes 31457280 | tf_op jit(solution)/shard_map/dot_general | solution.py:145
  541.2 43.0 %fusion.47 = f32[20,20]{1,0:T(8,128)S(1)} fusion(f32[20,2,3,32,2,512]{5,4,3,2,1,0:T(2,128)} %convert_multiply_fusion), kind=kOutput, calls=%fused_computation.59 | convolution fusion | flops 943718400 | bytes 15730240 | tf_op jit(solution)/shard_map/dot_general | solution.py:118
  588.2 9.9 %copy.92 = f32[2,16,3,32,32,2]{3,2,1,5,0,4:T(4,128)} copy(f32[2,16,3,32,32,2]{1,5,4,3,2,0:T(2,128)} %bitcast.193) | data formatting | bytes 1572864 | tf_op jit(solution)/shard_map/reshape | solution.py:108
  598.1 36.4 %fusion.42 = f32[2,3,32,2,512]{4,1,3,0,2:T(4,128)S(1)} fusion(f32[2,3,32,2,512]{4,1,3,0,2:T(4,128)} %copy-done, f32[2,16,3,32,32,2]{3,2,1,5,0,4:T(4,128)} %copy.92, f32[32,512,16,32,1,1]{1,3,2,5,4,0:T(8,128)} %bitcast.182, f32[32,512]{1,0:T(8,128)S(1)} %fusion.74), kind=kOutput, calls=%fused_computation.54 | convolution fusion | flops 1208549376 | bytes 35979264 | tf_op jit(solution)/shard_map/lwftsr,snwt->lfsrn/dot_general | solution.py:69
  636.5 22.9 %fusion.50 = f32[20]{0:T(128)S(1)} fusion(f32[20,2,3,32,2,512]{5,4,3,2,1,0:T(2,128)S(1)} %bitcast.184, f32[2,3,32,2,512,1]{4,1,3,0,2,5:T(4,128)S(1)} %bitcast.194), kind=kOutput, calls=%fused_computation.60 | convolution fusion | flops 47185920 | bytes 16515152 | tf_op jit(solution)/shard_map/dot_general | solution.py:93
  659.4 22.9 %fusion.53 = f32[20]{0:T(128)S(1)} fusion(f32[20,2,3,32,2,512]{5,4,3,2,1,0:T(2,128)S(1)} %bitcast.184, f32[2,3,32,2,512,1]{4,1,3,0,2,5:T(4,128)S(1)} %get-tuple-element.36), kind=kOutput, calls=%fused_computation.61 | convolution fusion | flops 47185920 | bytes 16515152 | tf_op jit(solution)/shard_map/dot_general | solution.py:93
  682.3 41.9 %all-reduce = (f32[]{:T(128)}, f32[20]{0:T(128)S(1)}, f32[20]{0:T(128)S(1)}, f32[]{:T(128)}, f32[]{:T(128)}, /*index=5*/f32[]{:T(128)}, f32[20,20]{1,0:T(8,128)S(1)}) all-reduce(f32[]{:T(128)} %get-tuple-element.43, f32[20]{0:T(128)S(1)} %fusion.53, f32[20]{0:T(128)S(1)} %fusion.50, ...), channel_id=1, replica_groups=mesh['wave'=16,'field'=2] {'wave','field'}, use_global_device_ids=true, to_apply=%region_3.4 | all-reduce | flops 444 | bytes 3552 | tf_op jit(solution)/shard_map/psum | solution.py:110
  731.2 24.4 %fusion.6 = f32[1,2,3,32,2,512]{5,0,4,3,2,1:T(1,128)S(1)} fusion(f32[2,3,32,2,512,20]{4,3,2,1,0,5:T(2,128)} %dot_general.57, f32[20]{0:T(128)S(1)} %get-tuple-element.33), kind=kOutput, calls=%fused_computation.6 | convolution fusion | flops 47185920 | bytes 16515152 | tf_op jit(solution)/shard_map/dot_general | solution.py:145
  (65 shorter events, 56.7 us)
Async XLA Ops:
  1.5 33.4 %copy-start.1 = (f32[2,3,32,2,512]{4,3,2,1,0:T(2,128)S(1)}, f32[2,3,32,2,512]{4,3,2,1,0:T(2,128)}, u32[]{:S(2)}) copy-start(f32[2,3,32,2,512]{4,3,2,1,0:T(2,128)} %param.10) | copy-start | bytes 2359300
  130.7 13.8 %copy-start.11 = (s32[512]{0:T(512)S(1)}, s32[512]{0:T(512)}, u32[]{:S(2)}) copy-start(s32[512]{0:T(512)} %param.15) | copy-start | bytes 6148
  130.7 13.9 %copy-start.10 = (bf16[3,3,32,1024]{3,2,1,0:T(8,128)(2,1)S(1)}, bf16[3,3,32,1024]{3,2,1,0:T(8,128)(2,1)}, u32[]{:S(2)}) copy-start(bf16[3,3,32,1024]{3,2,1,0:T(8,128)(2,1)} %param.18) | copy-start | bytes 1769476
  136.1 28.1 %all-to-all-start = ((f32[2,16,6144]{2,0,1:T(2,128)}), f32[2,16,6144]{2,0,1:T(2,128)}, u32[]{:S(2)}, u32[]{:S(2)}) async-start(f32[2,16,6144]{2,0,1:T(2,128)} %copy.75), calls=%async_computation | async-start | bytes 1572864 | tf_op jit(solution)/shard_map/all_to_all | solution.py:74
  188.3 1.6 copy-start.8
  188.3 2.2 copy-start.9
  218.5 24.5 %all-to-all-start.1 = ((f32[2,16,6144]{2,0,1:T(2,128)}), f32[2,16,6144]{2,0,1:T(2,128)}, u32[]{:S(2)}, u32[]{:S(2)}) async-start(f32[2,16,6144]{2,0,1:T(2,128)} %copy.80), calls=%async_computation.1 | async-start | bytes 1572864 | tf_op jit(solution)/shard_map/all_to_all | solution.py:84
  294.7 1.0 copy-start
  424.7 8.4 %copy-start.7 = (f32[16,32,2,1,1024]{4,1,0,2,3:T(8,128)S(1)}, f32[16,32,2,1,1024]{4,1,0,2,3:T(8,128)}, u32[]{:S(2)}) copy-start(f32[16,32,2,1,1024]{4,1,0,2,3:T(8,128)} %fusion.14) | copy-start | bytes 12582916
  432.7 2.2 copy-start.6
  468.8 115.4 %all-to-all-start.3 = ((f32[2,16,6144]{2,0,1:T(2,128)}), f32[2,16,6144]{2,0,1:T(2,128)S(1)}, u32[]{:S(2)}, u32[]{:S(2)}) async-start(f32[2,16,6144]{2,0,1:T(2,128)} %copy.90), calls=%async_computation.3 | async-start | bytes 1572864 | tf_op jit(solution)/shard_map/all_to_all | solution.py:105
  588.2 48.3 %slice-start = ((s8[15728640]{0:T(1024)(128)(4,1)}), s8[3145728]{0:T(1024)(128)(4,1)S(1)}, s32[]{:S(2)}) async-start(s8[15728640]{0:T(1024)(128)(4,1)} %bitcast.183), calls=%async_computation.4 | async-start | bytes 6291456
  598.1 36.4 %copy-start.2 = (f32[2,3,32,2,512]{4,3,2,1,0:T(2,128)S(1)}, f32[2,3,32,2,512]{4,3,2,1,0:T(2,128)}, u32[]{:S(2)}) copy-start(f32[2,3,32,2,512]{4,3,2,1,0:T(2,128)} %param.10) | copy-start | bytes 2359300
  598.1 38.4 %slice-start.1 = ((s8[15728640]{0:T(1024)(128)(4,1)}), s8[4194304]{0:T(1024)(128)(4,1)S(1)}, s32[]{:S(2)}) async-start(s8[15728640]{0:T(1024)(128)(4,1)} %bitcast.183), calls=%async_computation.5 | async-start | bytes 8388608
  598.1 38.4 %slice-start.2 = ((s8[15728640]{0:T(1024)(128)(4,1)}), s8[4194304]{0:T(1024)(128)(4,1)S(1)}, s32[]{:S(2)}) async-start(s8[15728640]{0:T(1024)(128)(4,1)} %bitcast.183), calls=%async_computation.6 | async-start | bytes 8388608
  598.1 38.4 %slice-start.3 = ((s8[15728640]{0:T(1024)(128)(4,1)}), s8[4194304]{0:T(1024)(128)(4,1)S(1)}, s32[]{:S(2)}) async-start(s8[15728640]{0:T(1024)(128)(4,1)} %bitcast.183), calls=%async_computation.7 | async-start | bytes 8388608
  634.6 24.8 %copy-start.4 = (f32[2,3,32,2,512]{4,1,3,0,2:T(4,128)}, f32[2,3,32,2,512]{4,1,3,0,2:T(4,128)S(1)}, u32[]{:S(2)}) copy-start(f32[2,3,32,2,512]{4,1,3,0,2:T(4,128)S(1)} %fusion.42) | copy-start | bytes 2359300
  728.4 27.2 %copy-start.12 = (f32[20]{0:T(128)}, f32[20]{0:T(128)S(1)}, u32[]{:S(2)}) copy-start(f32[20]{0:T(128)S(1)} %get-tuple-element.33) | copy-start | bytes 244
  731.1 24.5 %copy-start.3 = (f32[2,3,32,2,512]{4,3,2,1,0:T(2,128)S(1)}, f32[2,3,32,2,512]{4,3,2,1,0:T(2,128)}, u32[]{:S(2)}) copy-start(f32[2,3,32,2,512]{4,3,2,1,0:T(2,128)} %param.10) | copy-start | bytes 2359300
  731.2 24.5 %copy-start.5 = (f32[2,3,32,2,512]{4,1,3,0,2:T(4,128)S(1)}, f32[2,3,32,2,512]{4,1,3,0,2:T(4,128)}, u32[]{:S(2)}) copy-start(f32[2,3,32,2,512]{4,1,3,0,2:T(4,128)} %copy-done.4) | copy-start | bytes 2359300
where the time goes:
time: 767 us; the launch traced here: 761 us
  matrix products  399 us (52%)
  local copies, waits for them, and re-layouts  217 us (28%)
  blocking collectives  67.1 us (9%)
  other arithmetic  32.5 us (4%)
  waiting for transfers between devices  20.4 us (3%)
  starting transfers between devices  17.6 us (2%)
    dot_general x2, matrix products, to_latitudes(): jnp.einsum('lfsrn,snwt->lwftsr', spectral, blocked, precision=highest)  162 us
    dot_general x2, matrix products, to_degrees(): jnp.einsum('lwftsr,snwt->lfsrn', gathered, blocked, precision=highest)  73.4 us
    dot_general x2, matrix products, project(): return jnp.dot(kept_live, vector.reshape(-1), precision=highest)  45.8 us
    dot_general x1, matrix products, body(): jnp.dot(kept_live, kept_live.T, precision=highest)  43 us
    psum x1, blocking collectives, body(): lax.psum((jnp.sum(residual_left * residual_left), jnp.sum(adjoint_raw * a...  41.9 us
    unnamed x37, local copies, waits for them, and re-layouts  40.2 us
    reshape x1, local copies, waits for them, and re-layouts, body(): (kept_vectors.astype(jnp.float32) * wide_mask[None]).reshape(keep_count, -1)  30.3 us
    dot_general x1, local copies, waits for them, and re-layouts, body(): jnp.dot(correlations, kept_live, precision=highest)  29 us
  transfers between devices with their start and end apart: 3, of which 2 were waited for; matrix products, arithmetic and copies ran while one was open for 17% of the time, Pallas kernels for 0%

commit v1 on v0

v1 whole, which is shorter than its diff:
```python
import functools
import math

import jax
import jax.numpy as jnp
from jax import lax
from jax.experimental import pallas as pl
from jax.experimental.pallas import tpu as pltpu
from jax.sharding import PartitionSpec as P

time_step = 0.5
epsilon = 1e-06
f32 = jnp.float32
bf16 = jnp.bfloat16


def split(x):
    high = x.astype(bf16)
    return high, (x - high.astype(f32)).astype(bf16)


def dot(a, b, contract):
    return lax.dot_general(a, b, (((1,), (contract,)), ((), ())), preferred_element_type=f32)


def split_dot(rows, b_high, b_low, contract):
    count = rows.shape[0]
    high = rows.astype(bf16).astype(f32)
    both = jnp.concatenate([high, rows - high], axis=0).astype(bf16)
    upper = dot(both, b_high, contract)
    lower = dot(both[:count], b_low, contract)
    return upper[:count] + (upper[count:] + lower)


def table_kernel(longitudes, waves_ref, high_ref, low_ref):
    rows, width = high_ref.shape
    column = lax.broadcasted_iota(jnp.int32, (rows, width), 1)
    shift = jnp.where(pl.program_id(0) < pl.num_programs(0) // 2, 0, longitudes // 4)
    phase = lax.rem(waves_ref[...] * column + shift, longitudes)
    turn = phase.astype(f32) * (4.0 / longitudes)
    quadrant = jnp.floor(turn + 0.5)
    angle = (turn - quadrant) * (0.5 * math.pi)
    quadrant = quadrant.astype(jnp.int32) & 3
    square = angle * angle
    sine = angle * (
        1.0 + square * (-1 / 6 + square * (1 / 120 + square * (-1 / 5040 + square / 362880)))
    )
    cosine = 1.0 + square * (
        -0.5 + square * (1 / 24 + square * (-1 / 720 + square * (1 / 40320 - square / 3628800)))
    )
    value = jnp.where((quadrant & 1) == 1, sine, cosine)
    value = jnp.where((quadrant == 1) | (quadrant == 2), -value, value)
    high, low = split(value)
    high_ref[...] = high
    low_ref[...] = low


def fourier_table(wave_table, longitudes):
    slots = wave_table.shape[0]
    waves = jnp.concatenate([wave_table, wave_table])[:, None]
    block = slots // 4
    out = jax.ShapeDtypeStruct((2 * slots, longitudes), bf16)
    return pl.pallas_call(
        functools.partial(table_kernel, longitudes),
        grid=(8,),
        in_specs=[pl.BlockSpec((block, 1), lambda i: (i, 0))],
        out_specs=[pl.BlockSpec((block, longitudes), lambda i: (i, 0))] * 2,
        out_shape=[out, out],
        name="table",
    )(waves)


def legendre_kernel(mode, block, waves_ref, beta_ref, *refs):
    refs = list(refs)
    basis_ref = refs.pop(0)
    spectral_ref = refs.pop(0)
    prev_ref = refs.pop(0) if mode == "both" else None
    image_ref = refs.pop(0) if mode != "synthesis" else None
    new_ref = refs.pop(0) if mode != "synthesis" else None
    out_ref = refs.pop(0) if mode != "analysis" else None
    rows_ref = refs.pop(0)
    gather_ref = refs.pop(0) if mode != "synthesis" else None
    acc_ref = refs.pop(0) if mode != "analysis" else None
    levels, fields = spectral_ref.shape[:2]
    parts = spectral_ref.shape[3]
    degrees = basis_ref.shape[1]
    used = levels * fields * parts
    step = pl.program_id(0)
    waves_dev = pl.num_programs(0) * block

    @pl.when(step == 0)
    def _():
        rows_ref[...] = jnp.zeros_like(rows_ref)
        if gather_ref is not None:
            gather_ref[...] = image_ref[...].T

    for j in range(block):
        slot = step * block + j
        degree = lax.broadcasted_iota(jnp.int32, (rows_ref.shape[1], degrees), 1)
        mask = (degree >= waves_ref[slot]).astype(f32)

        def pack(which, ref):
            for l in range(levels):
                for f in range(fields):
                    at = (l * fields + f) * parts
                    rows_ref[which, pl.ds(at, parts), :] = ref[l, f, j]

        pack(0, spectral_ref)
        current = rows_ref[0] * mask
        high, low = split(basis_ref[j])
        if mode != "synthesis":
            for i in range(used):
                rows_ref[1, pl.ds(i, 1), :] = gather_ref[pl.ds(i * waves_dev + slot, 1), :]
            image = split_dot(rows_ref[1], high, low, 1) * mask
            current = current + time_step * image
            if mode == "both":
                pack(2, prev_ref)
                current = current - beta_ref[0] * (rows_ref[2] * mask)
            for l in range(levels):
                for f in range(fields):
                    at = (l * fields + f) * parts
                    new_ref[l, f, j] = current[at : at + parts]
        if mode != "analysis":
            result = split_dot(current, high, low, 0)
            for i in range(used):
                acc_ref[pl.ds(i * waves_dev + slot, 1), :] = result[i : i + 1]

    if mode != "analysis":

        @pl.when(step == pl.num_programs(0) - 1)
        def _():
            out_ref[...] = acc_ref[...].T


def legendre_call(mode, waves, beta, basis, spectral, prev=None, image=None):
    levels, fields, waves_dev, parts, degrees = spectral.shape
    latitudes = basis.shape[2]
    used = levels * fields * parts
    padded = -(-used // 16) * 16
    block = 2 if waves_dev % 2 == 0 else 1
    spec = pl.BlockSpec((levels, fields, block, parts, degrees), lambda s, *_: (0, 0, s, 0, 0))
    whole = pl.BlockSpec((latitudes, used * waves_dev), lambda s, *_: (0, 0))
    operands = [basis, spectral]
    in_specs = [pl.BlockSpec((block, degrees, latitudes), lambda s, *_: (s, 0, 0)), spec]
    out_specs, out_shape = [], []
    scratch = [pltpu.VMEM((3, padded, degrees), f32)]
    lanes = pltpu.VMEM((used * waves_dev, latitudes), f32)
    if mode == "both":
        operands.append(prev)
        in_specs.append(spec)
    if mode != "synthesis":
        operands.append(image)
        in_specs.append(whole)
        out_specs.append(spec)
        out_shape.append(jax.ShapeDtypeStruct(spectral.shape, f32))
        scratch.append(lanes)
    if mode != "analysis":
        out_specs.append(whole)
        out_shape.append(jax.ShapeDtypeStruct((latitudes, used * waves_dev), f32))
        scratch.append(lanes)
    return pl.pallas_call(
        functools.partial(legendre_kernel, mode, block),
        grid_spec=pltpu.PrefetchScalarGridSpec(
            num_scalar_prefetch=2,
            grid=(waves_dev // block,),
            in_specs=in_specs,
            out_specs=out_specs,
            scratch_shapes=scratch,
        ),
        out_shape=out_shape,
        compiler_params=pltpu.CompilerParams(vmem_limit_bytes=40 * 1024 * 1024),
        name=mode,
    )(waves, beta, *operands)


def fourier_kernel(
    adjoint, levels, fields, block_ref, scale_ref, weight_ref, high_ref, low_ref, value_ref,
    zonal_ref, out_ref, coef_ref, left_ref, right_ref, acc_ref,
):
    groups, lat_dev, columns = block_ref.shape
    items = levels * fields
    waves_dev = columns // (2 * items)
    slots = groups * waves_dev
    rows = items * lat_dev
    step = pl.program_id(0)

    @pl.when(step == 0)
    def _():
        for w in range(groups):
            for i in range(items):
                for r in range(2):
                    coef_ref[
                        pl.ds(i * lat_dev, lat_dev), pl.ds(r * slots + w * waves_dev, waves_dev)
                    ] = block_ref[w, :, pl.ds((2 * i + r) * waves_dev, waves_dev)]
        if not adjoint:
            scale = scale_ref[...]
            coef_ref[pl.ds(rows, rows), pl.ds(0, slots)] = (
                -scale * coef_ref[pl.ds(0, rows), pl.ds(slots, slots)]
            )
            coef_ref[pl.ds(rows, rows), pl.ds(slots, slots)] = (
                scale * coef_ref[pl.ds(0, rows), pl.ds(0, slots)]
            )
        acc_ref[...] = jnp.zeros_like(acc_ref)

    high, low = high_ref[...], low_ref[...]
    left_ref[...] = split_dot(coef_ref[...], high, low, 0)
    weight = weight_ref[...]
    for l in range(levels):
        base = l * fields
        if adjoint:
            grid = [left_ref[pl.ds((base + f) * lat_dev, lat_dev), :] * weight for f in range(fields)]
            for g in range(fields):
                for k, ref in enumerate((value_ref, zonal_ref)):
                    total = sum(ref[f, g].astype(f32) * grid[f] for f in range(fields))
                    right_ref[pl.ds(k * rows + (base + g) * lat_dev, lat_dev), :] = total
        else:
            value = [left_ref[pl.ds((base + g) * lat_dev, lat_dev), :] for g in range(fields)]
            slope = [left_ref[pl.ds(rows + (base + g) * lat_dev, lat_dev), :] for g in range(fields)]
            for f in range(fields):
                total = sum(
                    value_ref[f, g].astype(f32) * value[g] + zonal_ref[f, g].astype(f32) * slope[g]
                    for g in range(fields)
                )
                right_ref[pl.ds((base + f) * lat_dev, lat_dev), :] = total * weight
    acc_ref[...] += split_dot(right_ref[...], high, low, 1)

    @pl.when(step == pl.num_programs(0) - 1)
    def _():
        if adjoint:
            scale = scale_ref[...]
            first = pl.ds(0, rows)
            second = pl.ds(rows, rows)
            acc_ref[first, pl.ds(0, slots)] += scale * acc_ref[second, pl.ds(slots, slots)]
            acc_ref[first, pl.ds(slots, slots)] -= scale * acc_ref[second, pl.ds(0, slots)]
        for w in range(groups):
            for i in range(items):
                for r in range(2):
                    out_ref[w, :, pl.ds((2 * i + r) * waves_dev, waves_dev)] = acc_ref[
                        pl.ds(i * lat_dev, lat_dev), pl.ds(r * slots + w * waves_dev, waves_dev)
                    ]


def fourier_call(adjoint, levels, fields, block, scale, weight, table, value, zonal):
    groups, lat_dev, columns = block.shape
    high, low = table
    slots2, longitudes = high.shape
    chunk = 256
    rows = levels * fields * lat_dev
    before, after = (rows, 2 * rows) if adjoint else (2 * rows, rows)
    coef_spec = pl.BlockSpec((fields, fields, lat_dev, chunk), lambda c: (0, 0, 0, c))
    table_spec = pl.BlockSpec((slots2, chunk), lambda c: (0, c))
    block_spec = pl.BlockSpec(block.shape, lambda c: (0, 0, 0))
    return pl.pallas_call(
        functools.partial(fourier_kernel, adjoint, levels, fields),
        grid=(longitudes // chunk,),
        in_specs=[
            block_spec,
            pl.BlockSpec(scale.shape, lambda c: (0, 0)),
            pl.BlockSpec(weight.shape, lambda c: (0, 0)),
            table_spec,
            table_spec,
            coef_spec,
            coef_spec,
        ],
        out_specs=block_spec,
        out_shape=jax.ShapeDtypeStruct(block.shape, f32),
        scratch_shapes=[
            pltpu.VMEM((before, slots2), f32),
            pltpu.VMEM((before, chunk), f32),
            pltpu.VMEM((after, chunk), f32),
            pltpu.VMEM((after, slots2), f32),
        ],
        compiler_params=pltpu.CompilerParams(vmem_limit_bytes=40 * 1024 * 1024),
        name="adjoint" if adjoint else "forward",
    )(block, scale, weight, high, low, value, zonal)


def body(
    right_vector, left_prev, beta_prev, kept_vectors, kept_count, wave_table, legendre,
    quad_weights, coef_value, coef_zonal,
):
    levels, fields, waves_dev, _, degrees = right_vector.shape
    lat_dev, longitudes = coef_value.shape[2:]
    groups = lax.axis_size("wave")
    keep_count = kept_vectors.shape[0]
    entries = float(right_vector.size * groups * lax.axis_size("field"))
    device = lax.axis_index("wave")
    own_waves = lax.dynamic_slice_in_dim(wave_table, device * waves_dev, waves_dev)
    own_weights = lax.dynamic_slice_in_dim(quad_weights, device * lat_dev, lat_dev)
    weight = (own_weights * (degrees * longitudes) ** -0.5)[:, None]
    scale = (wave_table.astype(f32) / degrees)[None, :]
    table = fourier_table(wave_table, longitudes)
    degree_ids = jnp.arange(degrees, dtype=jnp.int32)
    live_mask = (degree_ids[None, :] >= own_waves[:, None]).astype(f32)[None, None, :, None, :]
    right_live = right_vector * live_mask

    def exchange(x):
        return lax.all_to_all(
            x.reshape(groups, lat_dev, -1), "wave", split_axis=0, concat_axis=0, tiled=True
        )

    def grid_pass(adjoint, latitude_part):
        block = exchange(latitude_part)
        block = fourier_call(
            adjoint, levels, fields, block, scale, weight, table, coef_value, coef_zonal
        )
        return exchange(block).reshape(groups * lat_dev, -1)

    (part,) = legendre_call("synthesis", own_waves, beta_prev, legendre, right_vector)
    image = grid_pass(False, part)
    residual_left, part = legendre_call(
        "both", own_waves, beta_prev, legendre, right_vector, left_prev, image
    )
    image = grid_pass(True, part)
    (adjoint_raw,) = legendre_call(
        "analysis", own_waves, beta_prev, legendre, residual_left, None, image
    )

    def project(vector):
        return jnp.sum(kept_vectors.astype(f32) * vector[None], axis=(1, 2, 3, 4, 5))

    sums = jnp.concatenate(
        [
            jnp.sum(residual_left * residual_left)[None],
            project(adjoint_raw),
            project(right_live),
        ]
    )
    sums = lax.psum(sums, ("wave", "field")) / entries
    alpha = jnp.sqrt(sums[0] + epsilon)
    live_flags = (jnp.arange(keep_count, dtype=jnp.int32) < kept_count[0]).astype(f32)
    correlations = (
        sums[1 : 1 + keep_count] / alpha - alpha * sums[1 + keep_count :]
    ) * live_flags
    correction = jnp.sum(
        kept_vectors.astype(f32) * correlations[:, None, None, None, None, None], axis=0
    )
    orthogonal = adjoint_raw / alpha - alpha * right_live - live_mask * correction
    square = lax.psum(jnp.sum(orthogonal * orthogonal), ("wave", "field")) / entries
    beta = jnp.sqrt(square + epsilon)
    return (residual_left / alpha, orthogonal / beta, correlations, jnp.stack([alpha, beta]))


def solution(mesh):
    spectral = P("field", None, "wave", None, None)
    grid = P(None, None, "wave", None)
    return jax.shard_map(
        body,
        mesh=mesh,
        in_specs=(
            spectral,
            spectral,
            P(),
            P(None, "field", None, "wave", None, None),
            P(),
            P(),
            P("wave", None, None),
            P(),
            grid,
            grid,
        ),
        out_specs=(spectral, spectral, P(), P()),
        check_vma=False,
    )
```

time: 767 us -> 318 us (0.41)
  matrix products: 399 us -> 0 us
  local copies, waits for them, and re-layouts: 217 us -> 7.36 us
  Pallas kernels: 0 us -> 99.4 us
  blocking collectives: 67.1 us -> 128 us
  other arithmetic: 32.5 us -> 46.3 us
    dot_general x13 -> x0, matrix products: 399 us -> none  [the longest x2 162 us: to_latitudes(): jnp.einsum('lfsrn,snwt->lwftsr', spectral, blocked, precision=highest)]
    pallas_call x0 -> x6, Pallas kernels: none -> 99.4 us  [the longest x3 66.4 us: legendre_call(): pl.pallas_call(functools.partial(legendre_kernel, mode, block), grid_spec...]
    reshape x9 -> x0, local copies, waits for them, and re-layouts: 89.6 us -> none  [the longest x1 30.3 us: body(): (kept_vectors.astype(jnp.float32) * wide_mask[None]).reshape(keep_count, -1)]
    reduce_sum x4, other arithmetic: 3.54 us -> 41.9 us  [the longest x1 25.8 us: project(): jnp.sum(kept_vectors.astype(f32) * vector[None], axis=(1, 2, 3, 4, 5))]
    transpose x4 -> x0, local copies, waits for them, and re-layouts: 38.1 us -> none  [the longest x2 19 us: to_latitudes(): jnp.einsum('lfsrn,snwt->lwftsr', spectral, blocked, precision=highest)]
    psum x1 -> x2, blocking collectives: 41.9 us -> 79.6 us  [the longest x1 39.8 us: body(): lax.psum(jnp.sum(orthogonal * orthogonal), ('wave', 'field')) / entries]
    unnamed x37 -> x28, local copies, waits for them, and re-layouts: 40.2 us -> 5.49 us
    dot_general x1 -> x0, local copies, waits for them, and re-layouts: 29 us -> none  [body(): jnp.dot(correlations, kept_live, precision=highest)]
  transfers between devices with their start and end apart: 3 -> 2, of which waited for: 2 -> 2; matrix products, arithmetic and copies ran while one was open for 17% -> 1% of each run, Pallas kernels for 0% -> 4%
where the time goes in v1:
time: 318 us; the launch traced here: 316 us
  blocking collectives  128 us (40%)
  Pallas kernels  99.4 us (31%)
  other arithmetic  46.3 us (15%)
  waiting for transfers between devices  20.2 us (6%)
  starting transfers between devices  12.1 us (4%)
  local copies, waits for them, and re-layouts  7.36 us (2%)
    pallas_call x3, Pallas kernels, legendre_call(): pl.pallas_call(functools.partial(legendre_kernel, mode, block), grid_spec...  66.4 us
    all_to_all x2, blocking collectives, exchange(): lax.all_to_all(x.reshape(groups, lat_dev, -1), 'wave', split_axis=0, conc...  48.4 us
    psum x1, blocking collectives, body(): lax.psum(jnp.sum(orthogonal * orthogonal), ('wave', 'field')) / entries  39.8 us
    psum x1, blocking collectives, body(): sums = lax.psum(sums, ('wave', 'field')) / entries  39.8 us
    reduce_sum x1, other arithmetic, project(): jnp.sum(kept_vectors.astype(f32) * vector[None], axis=(1, 2, 3, 4, 5))  25.8 us
    pallas_call x2, Pallas kernels, fourier_call(): pl.pallas_call(functools.partial(fourier_kernel, adjoint, levels, fields)...  20.5 us
    all_to_all x2, waiting for transfers between devices, exchange(): lax.all_to_all(x.reshape(groups, lat_dev, -1), 'wave', split_axis=0, conc...  20.2 us
    pallas_call x1, Pallas kernels, fourier_table(): pl.pallas_call(functools.partial(table_kernel, longitudes), grid=(8,), in...  12.5 us
  transfers between devices with their start and end apart: 2, of which 2 were waited for; matrix products, arithmetic and copies ran while one was open for 1% of the time, Pallas kernels for 4%

profile of v1, /device:TPU:0, one launch (start us, length us, event | category | flops | bytes accessed | tf_op | source)
XLA Modules:
  0.0 316.2 jit_solution(8906180620797036523)
XLA Ops:
  1.3 0.8 dynamic_slice.6.waves_ref
  2.0 1.1 copy-done
  3.2 20.0 %synthesis.1 = f32[512,384]{1,0:T(8,128)} custom-call(s32[32]{0:T(128)S(1)} %dynamic_slice.6.waves_ref, f32[1]{0:T(128)S(6)} %copy.19.beta_ref, f32[32,512,512]{2,1,0:T(8,128)} %refs_0_.5, f32[2,3,32,2,512]{4,3,2,1,0:T(2,128)S(1)} %copy-done), custom_call_target="tpu_custom_call" | custom-call | tf_op jit(solution)/shard_map/synthesis/pallas_call | solution.py:161
  23.2 8.3 %all-to-all-start = ((f32[16,32,384]{2,1,0:T(8,128)}), f32[16,32,384]{2,1,0:T(8,128)S(1)}, u32[]{:S(2)}, u32[]{:S(2)}) async-start(f32[16,32,384]{2,1,0:T(8,128)} %bitcast), calls=%async_computation | async-start | bytes 1572864 | tf_op jit(solution)/shard_map/all_to_all | solution.py:298
  31.5 0.8 multiply_bitcast_fusion
  32.3 0.1 copy.17.weight_ref
  32.4 1.0 copy.16.waves_ref
  33.4 12.5 %table.1 = (bf16[1024,1024]{1,0:T(8,128)(2,1)}, bf16[1024,1024]{1,0:T(8,128)(2,1)}) custom-call(s32[1024,1]{1,0:T(8,128)} %copy.16.waves_ref), custom_call_target="tpu_custom_call" | custom-call | tf_op jit(solution)/shard_map/table/pallas_call | solution.py:63
  46.0 5.3 %all-to-all-done.block_ref = f32[16,32,384]{2,1,0:T(8,128)S(1)} async-done(((f32[16,32,384]{2,1,0:T(8,128)}), f32[16,32,384]{2,1,0:T(8,128)S(1)}, u32[]{:S(2)}, u32[]{:S(2)}) %all-to-all-start) | async-done | bytes 786464 | tf_op jit(solution)/shard_map/all_to_all | solution.py:298
  51.2 1.6 copy-done.2
  52.8 1.6 copy-done.4
  54.4 9.9 %forward.1 = f32[16,32,384]{2,1,0:T(8,128)S(1)} custom-call(f32[16,32,384]{2,1,0:T(8,128)S(1)} %all-to-all-done.block_ref, f32[1,512]{1,0:T(1,128)S(1)} %bitcast.19, f32[32,1]{1,0:T(8,128)S(1)} %copy.17.weight_ref, bf16[1024,1024]{1,0:T(8,128)(2,1)S(1)} %copy-done.2, bf16[1024,1024]{1,0:T(8,128)(2,1)S(1)} %copy-done.4, ...), custom_call_target="tpu_custom_call" | custom-call | tf_op jit(solution)/shard_map/forward/pallas_call | solution.py:253
  64.4 25.0 %all_to_all.20 = f32[16,32,384]{2,1,0:T(8,128)S(1)} all-to-all(f32[16,32,384]{2,1,0:T(8,128)S(1)} %forward.1), channel_id=1, replica_groups=mesh['wave'=16,'field'=2] {'wave'}, dimensions={0} | all-to-all | bytes 1572864 | tf_op jit(solution)/shard_map/all_to_all | solution.py:298
  89.4 1.1 copy-done.8
  90.5 25.4 %both.1 = (f32[2,3,32,2,512]{4,3,2,1,0:T(2,128)S(1)}, f32[512,384]{1,0:T(8,128)S(1)}) custom-call(s32[32]{0:T(128)S(1)} %dynamic_slice.6.waves_ref, f32[1]{0:T(128)S(6)} %copy.19.beta_ref, f32[32,512,512]{2,1,0:T(8,128)} %refs_0_.5, f32[2,3,32,2,512]{4,3,2,1,0:T(2,128)S(1)} %copy-done.1, f32[2,3,32,2,512]{4,3,2,1,0:T(2,128)S(1)} %copy-done.8, ...), custom_call_target="tpu_custom_call" | custom-call | tf_op jit(solution)/shard_map/both/pallas_call | solution.py:161
  115.9 23.4 %all_to_all.21.block_ref = f32[16,32,384]{2,1,0:T(8,128)S(1)} all-to-all(f32[16,32,384]{2,1,0:T(8,128)S(1)} %bitcast.18), channel_id=1, replica_groups=mesh['wave'=16,'field'=2] {'wave'}, dimensions={0} | all-to-all | bytes 1572864 | tf_op jit(solution)/shard_map/all_to_all | solution.py:298
  139.3 10.5 %adjoint.1 = f32[16,32,384]{2,1,0:T(8,128)} custom-call(f32[16,32,384]{2,1,0:T(8,128)S(1)} %all_to_all.21.block_ref, f32[1,512]{1,0:T(1,128)S(1)} %bitcast.20, f32[32,1]{1,0:T(8,128)S(1)} %copy.17.weight_ref, bf16[1024,1024]{1,0:T(8,128)(2,1)S(1)} %copy-done.3, bf16[1024,1024]{1,0:T(8,128)(2,1)S(1)} %copy-done.5, bf16[3,3,32,1024]{3,2,1,0:T(8,128)(2,1)S(1)} %copy-done.6, ...), custom_call_target="tpu_custom_call" | custom-call | tf_op jit(solution)/shard_map/adjoint/pallas_call | solution.py:253
  149.9 3.8 %all-to-all-start.3 = ((f32[16,32,384]{2,1,0:T(8,128)}), f32[16,32,384]{2,1,0:T(8,128)S(1)}, u32[]{:S(2)}, u32[]{:S(2)}) async-start(f32[16,32,384]{2,1,0:T(8,128)} %adjoint.1), calls=%async_computation.3 | async-start | bytes 1572864 | tf_op jit(solution)/shard_map/all_to_all | solution.py:298
  154.3 0.1 fusion.4
  154.4 1.2 broadcast_multiply_fusion
  155.6 1.4 multiply_reduce_fusion.1
  157.0 14.9 %all-to-all-done.3 = f32[16,32,384]{2,1,0:T(8,128)S(1)} async-done(((f32[16,32,384]{2,1,0:T(8,128)}), f32[16,32,384]{2,1,0:T(8,128)S(1)}, u32[]{:S(2)}, u32[]{:S(2)}) %all-to-all-start.3) | async-done | bytes 786464 | tf_op jit(solution)/shard_map/all_to_all | solution.py:298
  171.9 21.0 %analysis.1 = f32[2,3,32,2,512]{4,3,2,1,0:T(2,128)S(1)} custom-call(s32[32]{0:T(128)S(1)} %dynamic_slice.6.waves_ref, f32[1]{0:T(128)S(6)} %copy.19.beta_ref, f32[32,512,512]{2,1,0:T(8,128)} %refs_0_.5, f32[2,3,32,2,512]{4,3,2,1,0:T(2,128)S(1)} %get-tuple-element.10.refs_1_, f32[512,384]{1,0:T(8,128)S(1)} %bitcast.16), custom_call_target="tpu_custom_call" | custom-call | tf_op jit(solution)/shard_map/analysis/pallas_call | solution.py:161
  193.0 25.8 %fusion = (f32[20]{0:T(128)S(1)}, f32[20]{0:T(128)S(1)}) fusion(bf16[20,2,3,32,2,512]{5,4,3,2,1,0:T(2,128)(2,1)} %param.13, f32[2,3,32,2,512]{4,3,2,1,0:T(2,128)S(1)} %analysis.1, f32[2,3,32,2,512]{4,3,2,1,0:T(2,128)S(1)} %copy-done.11), kind=kLoop, calls=%fused_computation.3 | loop fusion | flops 19660760 | bytes 9437344 | tf_op jit(solution)/shard_map/reduce_sum | solution.py:320
  218.8 0.7 pad_maximum_fusion
  219.5 39.8 %psum.14 = f32[41]{0:T(128)S(1)} all-reduce(f32[41]{0:T(128)S(1)} %pad_maximum_fusion), channel_id=1, replica_groups=mesh['wave'=16,'field'=2] {'wave','field'}, use_global_device_ids=true, to_apply=%region_3.0 | all-reduce | flops 41 | bytes 328 | tf_op jit(solution)/shard_map/psum | solution.py:329
  259.4 0.1 compare_select_fusion
  259.5 12.1 %fusion.2 = f32[2,3,32,2,512]{4,3,2,1,0:T(2,128)S(1)} fusion(bf16[20,2,3,32,2,512]{5,4,3,2,1,0:T(2,128)(2,1)} %param.13, f32[20]{0:T(128)S(1)} %compare_select_fusion), kind=kLoop, calls=%fused_computation.5 | loop fusion | flops 11599872 | bytes 8650832 | tf_op jit(solution)/shard_map/reduce_sum | solution.py:335
  271.5 2.6 multiply_reduce_fusion
  274.2 39.8 %psum.15 = f32[]{:T(128)} all-reduce(f32[]{:T(128)} %get-tuple-element.14), channel_id=1, replica_groups=mesh['wave'=16,'field'=2] {'wave','field'}, use_global_device_ids=true, to_apply=%region_6.0 | all-reduce | flops 1 | bytes 8 | tf_op jit(solution)/shard_map/psum | solution.py:339
  314.7 1.0 broadcast_divide_fusion
  315.6 0.6 pad_maximum_fusion.1
  (27 shorter events, 0.1 us)
Async XLA Ops:
  2.0 1.1 copy-start
  3.2 29.2 %copy-start.12 = (s32[512]{0:T(512)S(1)}, s32[512]{0:T(512)}, u32[]{:S(2)}) copy-start(s32[512]{0:T(512)} %param.15) | copy-start | bytes 6148
  3.2 48.0 %copy-start.6 = (bf16[3,3,32,1024]{3,2,1,0:T(8,128)(2,1)S(1)}, bf16[3,3,32,1024]{3,2,1,0:T(8,128)(2,1)}, u32[]{:S(2)}) copy-start(bf16[3,3,32,1024]{3,2,1,0:T(8,128)(2,1)} %value_ref.3) | copy-start | bytes 1769476
  3.2 48.0 %copy-start.7 = (bf16[3,3,32,1024]{3,2,1,0:T(8,128)(2,1)S(1)}, bf16[3,3,32,1024]{3,2,1,0:T(8,128)(2,1)}, u32[]{:S(2)}) copy-start(bf16[3,3,32,1024]{3,2,1,0:T(8,128)(2,1)} %zonal_ref.3) | copy-start | bytes 1769476
  3.2 86.2 %copy-start.1 = (f32[2,3,32,2,512]{4,3,2,1,0:T(2,128)S(1)}, f32[2,3,32,2,512]{4,3,2,1,0:T(2,128)}, u32[]{:S(2)}) copy-start(f32[2,3,32,2,512]{4,3,2,1,0:T(2,128)} %refs_1_.3) | copy-start | bytes 2359300
  23.2 28.0 %all-to-all-start = ((f32[16,32,384]{2,1,0:T(8,128)}), f32[16,32,384]{2,1,0:T(8,128)S(1)}, u32[]{:S(2)}, u32[]{:S(2)}) async-start(f32[16,32,384]{2,1,0:T(8,128)} %bitcast), calls=%async_computation | async-start | bytes 1572864 | tf_op jit(solution)/shard_map/all_to_all | solution.py:298
  46.0 43.4 %copy-start.9 = (f32[512]{0:T(512)}, f32[512]{0:T(512)S(1)}, u32[]{:S(2)}) copy-start(f32[512]{0:T(512)S(1)} %convert_multiply_fusion.3) | copy-start | bytes 6148
  51.2 1.6 copy-start.2
  52.8 1.6 copy-start.4
  89.4 1.1 copy-start.8
  90.5 48.8 %copy-start.3 = (bf16[1024,1024]{1,0:T(8,128)(2,1)S(1)}, bf16[1024,1024]{1,0:T(8,128)(2,1)}, u32[]{:S(2)}) copy-start(bf16[1024,1024]{1,0:T(8,128)(2,1)} %get-tuple-element.8.high_ref) | copy-start | bytes 6291460
  90.5 48.8 %copy-start.5 = (bf16[1024,1024]{1,0:T(8,128)(2,1)S(1)}, bf16[1024,1024]{1,0:T(8,128)(2,1)}, u32[]{:S(2)}) copy-start(bf16[1024,1024]{1,0:T(8,128)(2,1)} %get-tuple-element.9.low_ref) | copy-start | bytes 6291460
  90.5 48.8 %copy-start.10 = (f32[512]{0:T(512)S(1)}, f32[512]{0:T(512)}, u32[]{:S(2)}) copy-start(f32[512]{0:T(512)} %copy-done.9) | copy-start | bytes 6148
  149.9 22.0 %all-to-all-start.3 = ((f32[16,32,384]{2,1,0:T(8,128)}), f32[16,32,384]{2,1,0:T(8,128)S(1)}, u32[]{:S(2)}, u32[]{:S(2)}) async-start(f32[16,32,384]{2,1,0:T(8,128)} %adjoint.1), calls=%async_computation.3 | async-start | bytes 1572864 | tf_op jit(solution)/shard_map/all_to_all | solution.py:298
  171.9 21.1 %copy-start.11 = (f32[2,3,32,2,512]{4,3,2,1,0:T(2,128)S(1)}, f32[2,3,32,2,512]{4,3,2,1,0:T(2,128)}, u32[]{:S(2)}) copy-start(f32[2,3,32,2,512]{4,3,2,1,0:T(2,128)} %broadcast_multiply_fusion) | copy-start | bytes 2359300
  259.5 56.8 %copy-start.13 = (f32[20]{0:T(128)}, f32[20]{0:T(128)S(1)}, u32[]{:S(2)}) copy-start(f32[20]{0:T(128)S(1)} %compare_select_fusion) | copy-start | bytes 244

commit v2 on v1

--- a/solution.py
+++ b/solution.py
@@ -33,10 +33,11 @@
 
 
 def table_kernel(longitudes, waves_ref, high_ref, low_ref):
-    rows, width = high_ref.shape
+    _, rows, width = high_ref.shape
     column = lax.broadcasted_iota(jnp.int32, (rows, width), 1)
-    shift = jnp.where(pl.program_id(0) < pl.num_programs(0) // 2, 0, longitudes // 4)
-    phase = lax.rem(waves_ref[...] * column + shift, longitudes)
+    phase = waves_ref[...] * column
+    if longitudes & (longitudes - 1):
+        phase = lax.rem(phase, longitudes)
     turn = phase.astype(f32) * (4.0 / longitudes)
     quadrant = jnp.floor(turn + 0.5)
     angle = (turn - quadrant) * (0.5 * math.pi)
@@ -48,33 +49,148 @@
     cosine = 1.0 + square * (
         -0.5 + square * (1 / 24 + square * (-1 / 720 + square * (1 / 40320 - square / 3628800)))
     )
-    value = jnp.where((quadrant & 1) == 1, sine, cosine)
-    value = jnp.where((quadrant == 1) | (quadrant == 2), -value, value)
-    high, low = split(value)
-    high_ref[...] = high
-    low_ref[...] = low
+    odd = (quadrant & 1) == 1
+    turned = jnp.where(odd, sine, cosine)
+    turned = jnp.where((quadrant == 1) | (quadrant == 2), -turned, turned)
+    minus_sine = jnp.where(odd, cosine, sine)
+    minus_sine = jnp.where(quadrant < 2, -minus_sine, minus_sine)
+    for r, value in enumerate((turned, minus_sine)):
+        high, low = split(value)
+        high_ref[r] = high
+        low_ref[r] = low
 
 
 def fourier_table(wave_table, longitudes):
     slots = wave_table.shape[0]
-    waves = jnp.concatenate([wave_table, wave_table])[:, None]
     block = slots // 4
-    out = jax.ShapeDtypeStruct((2 * slots, longitudes), bf16)
-    return pl.pallas_call(
+    out = jax.ShapeDtypeStruct((2, slots, longitudes), bf16)
+    parts = pl.pallas_call(
         functools.partial(table_kernel, longitudes),
-        grid=(8,),
+        grid=(4,),
         in_specs=[pl.BlockSpec((block, 1), lambda i: (i, 0))],
-        out_specs=[pl.BlockSpec((block, longitudes), lambda i: (i, 0))] * 2,
+        out_specs=[pl.BlockSpec((2, block, longitudes), lambda i: (0, i, 0))] * 2,
         out_shape=[out, out],
         name="table",
-    )(waves)
+    )(wave_table[:, None])
+    return [part.reshape(2 * slots, longitudes) for part in parts]
+
+
+def loop(count, visit):
+    def at(index, carry):
+        visit(index)
+        return carry
+
+    lax.fori_loop(1, count, at, 0)
+
+
+def exchange_kernel(blocks, sums, *refs):
+    refs = list(refs)
+    block_ref = refs.pop(0) if blocks else None
+    row_ref = refs.pop(0) if sums else None
+    out_ref = refs.pop(0) if blocks else None
+    total_ref = refs.pop(0) if sums else None
+    wave, field = lax.axis_index("wave"), lax.axis_index("field")
+    groups, cores = lax.axis_size("wave"), lax.axis_size("field")
+    count = groups * cores
+    me = wave * cores + field
+
+    def device(index):
+        return {"wave": lax.div(index, cores), "field": lax.rem(index, cores)}
+
+    barrier = pltpu.get_barrier_semaphore()
+    if sums:
+        loop(count, lambda d: pl.semaphore_signal(
+            barrier, inc=1, device_id=device(lax.rem(me + d, count)),
+            device_id_type=pl.DeviceIdType.MESH))
+        pl.semaphore_wait(barrier, count - 1)
+    else:
+        loop(groups, lambda d: pl.semaphore_signal(
+            barrier, inc=1, device_id={"wave": lax.rem(wave + d, groups)},
+            device_id_type=pl.DeviceIdType.MESH))
+        pl.semaphore_wait(barrier, groups - 1)
+    if sums:
+        slots, row_send, row_recv = refs[-3:]
+
+        def row_copy(peer, slot):
+            return pltpu.make_async_remote_copy(
+                src_ref=row_ref, dst_ref=slots.at[slot], send_sem=row_send.at[peer],
+                recv_sem=row_recv.at[slot], device_id=device(peer),
+                device_id_type=pl.DeviceIdType.MESH)
+
+        loop(count, lambda d: row_copy(lax.rem(me + d, count), me).start())
+    if blocks:
+        local, send, recv = refs[:3]
+
+        def block_copy(peer, slot):
+            return pltpu.make_async_remote_copy(
+                src_ref=block_ref.at[peer], dst_ref=out_ref.at[slot], send_sem=send.at[peer],
+                recv_sem=recv.at[slot], device_id={"wave": peer},
+                device_id_type=pl.DeviceIdType.MESH)
+
+        loop(groups, lambda d: block_copy(lax.rem(wave + d, groups), wave).start())
+        own = pltpu.make_async_copy(block_ref.at[wave], out_ref.at[wave], local)
+        own.start()
+    if sums:
+        slots[me] = row_ref[...]
+
+        def row_wait(d):
+            peer = lax.rem(me + d, count)
+            row_copy(peer, peer).wait_recv()
+            row_copy(peer, peer).wait_send()
+
+        loop(count, row_wait)
+        total_ref[...] = jnp.sum(slots[...], axis=0)
+    if blocks:
+
+        def block_wait(d):
+            peer = lax.rem(wave + d, groups)
+            block_copy(peer, peer).wait_recv()
+            block_copy(peer, peer).wait_send()
+
+        loop(groups, block_wait)
+        own.wait()
+
+
+def exchange_call(identity, block=None, sums=None):
+    groups, cores = lax.axis_size("wave"), lax.axis_size("field")
+    operands, in_specs, out_specs, out_shape, scratch = [], [], [], [], []
+    if block is not None:
+        operands.append(block)
+        in_specs.append(pl.BlockSpec(memory_space=pl.ANY))
+        out_specs.append(pl.BlockSpec(memory_space=pl.ANY))
+        out_shape.append(jax.ShapeDtypeStruct(block.shape, f32))
+        scratch += [
+            pltpu.SemaphoreType.DMA,
+            pltpu.SemaphoreType.DMA((groups,)),
+            pltpu.SemaphoreType.DMA((groups,)),
+        ]
+    if sums is not None:
+        row = jnp.pad(sums, (0, 128 - sums.shape[0]))[None]
+        operands.append(row)
+        in_specs.append(pl.BlockSpec(memory_space=pltpu.VMEM))
+        out_specs.append(pl.BlockSpec(memory_space=pltpu.VMEM))
+        out_shape.append(jax.ShapeDtypeStruct(row.shape, f32))
+        scratch += [
+            pltpu.VMEM((groups * cores,) + row.shape, f32),
+            pltpu.SemaphoreType.DMA((groups * cores,)),
+            pltpu.SemaphoreType.DMA((groups * cores,)),
+        ]
+    return pl.pallas_call(
+        functools.partial(exchange_kernel, block is not None, sums is not None),
+        in_specs=in_specs,
+        out_specs=out_specs,
+        out_shape=out_shape,
+        scratch_shapes=scratch,
+        compiler_params=pltpu.CompilerParams(collective_id=identity, has_side_effects=True),
+        name=f"exchange_{identity}",
+    )(*operands)
 
 
 def legendre_kernel(mode, block, waves_ref, beta_ref, *refs):
     refs = list(refs)
     basis_ref = refs.pop(0)
     spectral_ref = refs.pop(0)
-    prev_ref = refs.pop(0) if mode == "both" else None
+    prev_ref = refs.pop(0) if mode != "synthesis" else None
     image_ref = refs.pop(0) if mode != "synthesis" else None
     new_ref = refs.pop(0) if mode != "synthesis" else None
     out_ref = refs.pop(0) if mode != "analysis" else None
@@ -113,9 +229,11 @@
                 rows_ref[1, pl.ds(i, 1), :] = gather_ref[pl.ds(i * waves_dev + slot, 1), :]
             image = split_dot(rows_ref[1], high, low, 1) * mask
             current = current + time_step * image
+            pack(2, prev_ref)
             if mode == "both":
-                pack(2, prev_ref)
                 current = current - beta_ref[0] * (rows_ref[2] * mask)
+            else:
+                current = current / beta_ref[0] - beta_ref[0] * (rows_ref[2] * mask)
             for l in range(levels):
                 for f in range(fields):
                     at = (l * fields + f) * parts
@@ -145,7 +263,7 @@
     out_specs, out_shape = [], []
     scratch = [pltpu.VMEM((3, padded, degrees), f32)]
     lanes = pltpu.VMEM((used * waves_dev, latitudes), f32)
-    if mode == "both":
+    if mode != "synthesis":
         operands.append(prev)
         in_specs.append(spec)
     if mode != "synthesis":
@@ -292,52 +410,40 @@
     table = fourier_table(wave_table, longitudes)
     degree_ids = jnp.arange(degrees, dtype=jnp.int32)
     live_mask = (degree_ids[None, :] >= own_waves[:, None]).astype(f32)[None, None, :, None, :]
-    right_live = right_vector * live_mask
-
-    def exchange(x):
-        return lax.all_to_all(
-            x.reshape(groups, lat_dev, -1), "wave", split_axis=0, concat_axis=0, tiled=True
-        )
-
-    def grid_pass(adjoint, latitude_part):
-        block = exchange(latitude_part)
-        block = fourier_call(
+
+    def grid_blocks(part):
+        return part.reshape(groups, lat_dev, -1)
+
+    def grid_pass(adjoint, block):
+        return fourier_call(
             adjoint, levels, fields, block, scale, weight, table, coef_value, coef_zonal
         )
-        return exchange(block).reshape(groups * lat_dev, -1)
 
     (part,) = legendre_call("synthesis", own_waves, beta_prev, legendre, right_vector)
-    image = grid_pass(False, part)
+    (block,) = exchange_call(0, grid_blocks(part))
+    (block,) = exchange_call(1, grid_pass(False, block))
     residual_left, part = legendre_call(
-        "both", own_waves, beta_prev, legendre, right_vector, left_prev, image
-    )
-    image = grid_pass(True, part)
-    (adjoint_raw,) = legendre_call(
-        "analysis", own_waves, beta_prev, legendre, residual_left, None, image
-    )
-
-    def project(vector):
-        return jnp.sum(kept_vectors.astype(f32) * vector[None], axis=(1, 2, 3, 4, 5))
-
-    sums = jnp.concatenate(
-        [
-            jnp.sum(residual_left * residual_left)[None],
-            project(adjoint_raw),
-            project(right_live),
-        ]
-    )
-    sums = lax.psum(sums, ("wave", "field")) / entries
-    alpha = jnp.sqrt(sums[0] + epsilon)
+        "both", own_waves, beta_prev, legendre, right_vector, left_prev,
+        block.reshape(groups * lat_dev, -1),
+    )
+    square = jnp.sum(residual_left * residual_left)[None]
+    block, sums = exchange_call(2, grid_blocks(part), square)
+    alpha = jnp.sqrt(sums[0, 0] / entries + epsilon)
+    (block,) = exchange_call(3, grid_pass(True, block))
+    (candidate,) = legendre_call(
+        "analysis", own_waves, alpha[None], legendre, residual_left, right_vector,
+        block.reshape(groups * lat_dev, -1),
+    )
+    raw = jnp.sum(kept_vectors.astype(f32) * candidate[None], axis=(1, 2, 3, 4, 5))
+    (sums,) = exchange_call(4, sums=raw)
     live_flags = (jnp.arange(keep_count, dtype=jnp.int32) < kept_count[0]).astype(f32)
-    correlations = (
-        sums[1 : 1 + keep_count] / alpha - alpha * sums[1 + keep_count :]
-    ) * live_flags
+    correlations = sums[0, :keep_count] / entries * live_flags
     correction = jnp.sum(
         kept_vectors.astype(f32) * correlations[:, None, None, None, None, None], axis=0
     )
-    orthogonal = adjoint_raw / alpha - alpha * right_live - live_mask * correction
-    square = lax.psum(jnp.sum(orthogonal * orthogonal), ("wave", "field")) / entries
-    beta = jnp.sqrt(square + epsilon)
+    orthogonal = candidate - live_mask * correction
+    (sums,) = exchange_call(5, sums=jnp.sum(orthogonal * orthogonal)[None])
+    beta = jnp.sqrt(sums[0, 0] / entries + epsilon)
     return (residual_left / alpha, orthogonal / beta, correlations, jnp.stack([alpha, beta]))
 
 

time: 318 us -> 264 us (0.83)
  blocking collectives: 128 us -> 0 us
  Pallas kernels: 99.4 us -> 206 us
  waiting for transfers between devices: 20.2 us -> 0 us
  other arithmetic: 46.3 us -> 30.5 us
  local copies, waits for them, and re-layouts: 7.36 us -> 22.9 us
  starting transfers between devices: 12.1 us -> 0 us
    pallas_call x1 -> x7, Pallas kernels: 12.5 us -> 121 us  [the longest x6 113 us: exchange_call(): pl.pallas_call(functools.partial(exchange_kernel, block is not None, sums...]
    psum x2 -> x0, blocking collectives: 79.6 us -> none  [the longest x1 39.8 us: body(): lax.psum(jnp.sum(orthogonal * orthogonal), ('wave', 'field')) / entries]
    all_to_all x2 -> x0, blocking collectives: 48.4 us -> none  [exchange(): lax.all_to_all(x.reshape(groups, lat_dev, -1), 'wave', split_axis=0, conc...]
    all_to_all x2 -> x0, waiting for transfers between devices: 20.2 us -> none  [exchange(): lax.all_to_all(x.reshape(groups, lat_dev, -1), 'wave', split_axis=0, conc...]
    reduce_sum x3, other arithmetic: 29.9 us -> 14.3 us  [the longest x1 11.5 us: body(): jnp.sum(kept_vectors.astype(f32) * candidate[None], axis=(1, 2, 3, 4, 5))]
    unnamed x28 -> x42, local copies, waits for them, and re-layouts: 5.49 us -> 18.4 us
    all_to_all x2 -> x0, starting transfers between devices: 12.1 us -> none  [exchange(): lax.all_to_all(x.reshape(groups, lat_dev, -1), 'wave', split_axis=0, conc...]
  transfers between devices with their start and end apart: 2 -> 0, of which waited for: 2 -> 0; matrix products, arithmetic and copies ran while one was open for 1% -> 0% of each run, Pallas kernels for 4% -> 0%
where the time goes in v2:
time: 264 us; the launch traced here: 263 us
  Pallas kernels  206 us (78%)
  other arithmetic  30.5 us (12%)
  local copies, waits for them, and re-layouts  22.9 us (9%)
  between operations  3.42 us (1%)
    pallas_call x6, Pallas kernels, exchange_call(): pl.pallas_call(functools.partial(exchange_kernel, block is not None, sums...  113 us
    pallas_call x3, Pallas kernels, legendre_call(): pl.pallas_call(functools.partial(legendre_kernel, mode, block), grid_spec...  65.4 us
    pallas_call x2, Pallas kernels, fourier_call(): pl.pallas_call(functools.partial(fourier_kernel, adjoint, levels, fields)...  19.6 us
    unnamed x42, local copies, waits for them, and re-layouts  18.4 us
    reduce_sum x1, other arithmetic, body(): jnp.sum(kept_vectors.astype(f32) * correlations[:, None, None, None, None...  12.3 us
    reduce_sum x1, other arithmetic, body(): jnp.sum(kept_vectors.astype(f32) * candidate[None], axis=(1, 2, 3, 4, 5))  11.5 us
    pallas_call x1, Pallas kernels, fourier_table(): pl.pallas_call(functools.partial(table_kernel, longitudes), grid=(4,), in...  7.91 us

profile of v2, /device:TPU:0, one launch (start us, length us, event | category | flops | bytes accessed | tf_op | source)
XLA Modules:
  0.0 262.5 jit_solution(2049231588462466707)
XLA Ops:
  2.1 1.1 copy-done.4
  3.2 19.0 %synthesis.1 = f32[512,384]{1,0:T(8,128)S(1)} custom-call(s32[32]{0:T(128)S(1)} %dynamic_slice.6.waves_ref, f32[1]{0:T(128)S(6)} %copy.19.beta_ref, f32[32,512,512]{2,1,0:T(8,128)} %refs_0_.5, f32[2,3,32,2,512]{4,3,2,1,0:T(2,128)S(1)} %copy-done.4), custom_call_target="tpu_custom_call" | custom-call | tf_op jit(solution)/shard_map/synthesis/pallas_call | solution.py:279
  22.3 0.9 copy-done.11
  23.1 20.2 %exchange_0.1.block_ref = f32[16,32,384]{2,1,0:T(8,128)} custom-call(f32[16,32,384]{2,1,0:T(8,128)} %bitcast.33), custom_call_target="tpu_custom_call" | custom-call | tf_op jit(solution)/shard_map/exchange_0/pallas_call | solution.py:178
  45.1 7.9 %table.1 = (bf16[2,512,1024]{2,1,0:T(8,128)(2,1)}, bf16[2,512,1024]{2,1,0:T(8,128)(2,1)}) custom-call(s32[512,1]{1,0:T(8,128)} %copy.16.waves_ref), custom_call_target="tpu_custom_call" | custom-call | tf_op jit(solution)/shard_map/table/pallas_call | solution.py:67
  53.0 1.6 copy-done
  54.6 1.6 copy-done.2
  56.2 1.1 copy-done.7
  57.3 9.9 %forward.1.refs_0_ = f32[16,32,384]{2,1,0:T(8,128)S(1)} custom-call(f32[16,32,384]{2,1,0:T(8,128)S(1)} %copy-done.7, f32[1,512]{1,0:T(1,128)S(1)} %bitcast.36, f32[32,1]{1,0:T(8,128)S(1)} %copy.17.weight_ref, bf16[1024,1024]{1,0:T(8,128)(2,1)S(1)} %bitcast.28, bf16[1024,1024]{1,0:T(8,128)(2,1)S(1)} %bitcast.30, bf16[3,3,32,1024]{3,2,1,0:T(8,128)(2,1)S(1)} %copy-done.13, ...), custom_call_target="tpu_custom_call" | custom-call | tf_op jit(solution)/shard_map/forward/pallas_call | solution.py:371
  68.1 21.6 %exchange_1.1 = f32[16,32,384]{2,1,0:T(8,128)} custom-call(f32[16,32,384]{2,1,0:T(8,128)} %copy-done.9), custom_call_target="tpu_custom_call" | custom-call | tf_op jit(solution)/shard_map/exchange_1/pallas_call | solution.py:178
  89.8 1.1 copy-done.5
  90.9 1.1 copy-done.12
  92.0 1.1 copy-done.18
  93.2 25.2 %both.1 = (f32[2,3,32,2,512]{4,3,2,1,0:T(2,128)S(1)}, f32[512,384]{1,0:T(8,128)S(1)}) custom-call(s32[32]{0:T(128)S(1)} %dynamic_slice.6.waves_ref, f32[1]{0:T(128)S(6)} %copy.19.beta_ref, f32[32,512,512]{2,1,0:T(8,128)} %refs_0_.5, f32[2,3,32,2,512]{4,3,2,1,0:T(2,128)S(1)} %copy-done.5, f32[2,3,32,2,512]{4,3,2,1,0:T(2,128)S(1)} %copy-done.18, ...), custom_call_target="tpu_custom_call" | custom-call | tf_op jit(solution)/shard_map/both/pallas_call | solution.py:279
  119.3 1.4 multiply_reduce_fusion.1
  120.7 1.2 pad_bitcast_fusion.2.refs_1_
  121.8 25.4 %exchange_2.1 = (f32[16,32,384]{2,1,0:T(8,128)}, f32[1,128]{1,0:T(1,128)}) custom-call(f32[16,32,384]{2,1,0:T(8,128)} %bitcast.35, f32[1,128]{1,0:T(1,128)} %pad_bitcast_fusion.2.refs_1_), custom_call_target="tpu_custom_call" | custom-call | tf_op jit(solution)/shard_map/exchange_2/pallas_call | solution.py:178
  147.2 1.6 copy-done.3
  148.8 1.1 copy-done.15
  149.9 1.1 copy-done.16
  151.0 9.6 %adjoint.1.refs_0_ = f32[16,32,384]{2,1,0:T(8,128)S(1)} custom-call(f32[16,32,384]{2,1,0:T(8,128)S(1)} %copy-done.16, f32[1,512]{1,0:T(1,128)S(1)} %bitcast.37, f32[32,1]{1,0:T(8,128)S(1)} %copy.17.weight_ref, bf16[1024,1024]{1,0:T(8,128)(2,1)S(1)} %bitcast.29, bf16[1024,1024]{1,0:T(8,128)(2,1)S(1)} %bitcast.31, bf16[3,3,32,1024]{3,2,1,0:T(8,128)(2,1)S(1)} %copy-done.13, ...), custom_call_target="tpu_custom_call" | custom-call | tf_op jit(solution)/shard_map/adjoint/pallas_call | solution.py:371
  161.5 22.6 %exchange_3.1 = f32[16,32,384]{2,1,0:T(8,128)} custom-call(f32[16,32,384]{2,1,0:T(8,128)} %copy-done.8), custom_call_target="tpu_custom_call" | custom-call | tf_op jit(solution)/shard_map/exchange_3/pallas_call | solution.py:178
  184.8 1.1 copy-done.6
  185.9 1.1 copy-done.10
  187.1 21.2 %analysis.1 = f32[2,3,32,2,512]{4,3,2,1,0:T(2,128)S(1)} custom-call(s32[32]{0:T(128)S(1)} %dynamic_slice.6.waves_ref, f32[1]{0:T(128)} %bitcast.11.beta_ref, f32[32,512,512]{2,1,0:T(8,128)} %refs_0_.5, f32[2,3,32,2,512]{4,3,2,1,0:T(2,128)S(1)} %get-tuple-element.12.refs_1_, f32[2,3,32,2,512]{4,3,2,1,0:T(2,128)S(1)} %copy-done.6, f32[512,384]{1,0:T(8,128)S(1)} %bitcast.32), custom_call_target="tpu_custom_call" | custom-call | tf_op jit(solution)/shard_map/analysis/pallas_call | solution.py:279
  208.2 11.5 %fusion = f32[20]{0:T(128)S(1)} fusion(bf16[20,2,3,32,2,512]{5,4,3,2,1,0:T(2,128)(2,1)} %param.13, f32[2,3,32,2,512]{4,3,2,1,0:T(2,128)S(1)} %analysis.1), kind=kLoop, calls=%fused_computation.2 | loop fusion | flops 11796460 | bytes 8650832 | tf_op jit(solution)/shard_map/reduce_sum | solution.py:437
  220.3 13.7 %exchange_4.1 = f32[1,128]{1,0:T(1,128)} custom-call(f32[1,128]{1,0:T(1,128)} %pad_bitcast_fusion.1.refs_0_), custom_call_target="tpu_custom_call" | custom-call | tf_op jit(solution)/shard_map/exchange_4/pallas_call | solution.py:178
  235.2 12.3 %fusion.1 = f32[2,3,32,2,512]{4,3,2,1,0:T(2,128)S(1)} fusion(bf16[20,2,3,32,2,512]{5,4,3,2,1,0:T(2,128)(2,1)} %param.13, f32[20]{0:T(128)S(1)} %compare_select_fusion), kind=kLoop, calls=%fused_computation.3 | loop fusion | flops 11599872 | bytes 8650832 | tf_op jit(solution)/shard_map/reduce_sum | solution.py:441
  247.6 1.4 multiply_reduce_fusion
  249.0 1.2 pad_bitcast_fusion.refs_0_
  250.1 9.3 %exchange_5.1 = f32[1,128]{1,0:T(1,128)} custom-call(f32[1,128]{1,0:T(1,128)} %pad_bitcast_fusion.refs_0_), custom_call_target="tpu_custom_call" | custom-call | tf_op jit(solution)/shard_map/exchange_5/pallas_call | solution.py:178
  260.7 1.8 broadcast_divide_fusion
  (38 shorter events, 6.9 us)
Async XLA Ops:
  2.0 1.1 copy-start.4
  3.2 41.0 %copy-start.19 = (s32[512]{0:T(512)S(1)}, s32[512]{0:T(512)}, u32[]{:S(2)}) copy-start(s32[512]{0:T(512)} %param.15) | copy-start | bytes 6148
  3.2 49.8 %copy-start.13 = (bf16[3,3,32,1024]{3,2,1,0:T(8,128)(2,1)S(1)}, bf16[3,3,32,1024]{3,2,1,0:T(8,128)(2,1)}, u32[]{:S(2)}) copy-start(bf16[3,3,32,1024]{3,2,1,0:T(8,128)(2,1)} %value_ref.3) | copy-start | bytes 1769476
  3.2 49.8 %copy-start.14 = (bf16[3,3,32,1024]{3,2,1,0:T(8,128)(2,1)S(1)}, bf16[3,3,32,1024]{3,2,1,0:T(8,128)(2,1)}, u32[]{:S(2)}) copy-start(bf16[3,3,32,1024]{3,2,1,0:T(8,128)(2,1)} %zonal_ref.3) | copy-start | bytes 1769476
  22.2 0.9 copy-start.11
  53.0 1.6 copy-start
  54.6 1.6 copy-start.2
  56.2 1.1 copy-start.7
  67.3 0.9 copy-start.9
  89.7 1.1 copy-start.5
  90.9 1.1 copy-start.12
  92.0 1.1 copy-start.18
  93.2 54.1 %copy-start.1 = (bf16[2,512,1024]{2,1,0:T(8,128)(2,1)S(1)}, bf16[2,512,1024]{2,1,0:T(8,128)(2,1)}, u32[]{:S(2)}) copy-start(bf16[2,512,1024]{2,1,0:T(8,128)(2,1)} %get-tuple-element.10) | copy-start | bytes 6291460
  118.4 0.9 copy-start.17
  147.2 1.6 copy-start.3
  148.8 1.1 copy-start.15
  149.9 1.1 copy-start.16
  160.6 0.9 copy-start.8
  184.8 1.1 copy-start.6
  185.9 1.1 copy-start.10
  235.2 27.3 %copy-start.20 = (f32[20]{0:T(128)}, f32[20]{0:T(128)S(1)}, u32[]{:S(2)}) copy-start(f32[20]{0:T(128)S(1)} %compare_select_fusion) | copy-start | bytes 244
